TPU v7x, 512 devices: a whole 4x4x16 slice. The times are simulated.
512 devices in a mesh: seg: 32 (over x, z_hi, core), bond: 16 (over z_lo, y).
Axes of the slice: x: 4, y: 4, z: 16 (z_hi: 4, z_lo: 4; z = z_hi * 4 + z_lo), core: 2. Of those that a mesh axis runs over, the one named last changes fastest.
Arguments:
- left_env: bfloat16 [32, 128, 128, 128], P('seg', None, 'bond'), may hold values from -1 to 1, as said below
- right_env: bfloat16 [32, 128, 128, 128], P('seg', None, 'bond'), may hold values from -1 to 1, as said below
- mpo_site: bfloat16 [32, 128, 8, 8, 8], P('seg', 'bond'), may hold values from -1 to 1, as said below
- start_state: bfloat16 [32, 128, 8, 128], P('seg'), may hold values from -6 to 6
Outputs:
- new_state: bfloat16 [32, 128, 8, 128], P('seg')
- new_left: bfloat16 [32, 128, 128, 128], P('seg', None, 'bond')
- energy: float32 [32], P('seg')
- second_image: float32 [32, 128, 8, 128], P('seg', 'bond')
Inputs may be any that keep to these rules, and one draw needn't show every extreme that they name: left_env[s, a, w, c] equals left_env[s, c, w, a]. right_env[s, b, w, c] equals right_env[s, c, w, b]. mpo_site[s, w, u, i, j] equals mpo_site[s, w, u, j, i].
All inputs are finite; a program needn't handle non-finite values.
Results may differ from a plain program's by a relative error of at most 0.01.
Values may be sent and summed in bfloat16 or wider, within the bound.
A program may use at most 64 MiB of HBM per device.

v0:
```python
import jax
import jax.numpy as jnp
from jax import lax
from jax.sharding import PartitionSpec as P

epsilon = 1e-06


def shifted(value, axis, steps):
    count = lax.axis_size(axis)
    pairs = [(source, (source + steps) % count) for source in range(count)]
    return lax.ppermute(value, axis, pairs)


def first_section(left_block, vector):
    height, width_block = (left_block.shape[0], left_block.shape[1])
    return jnp.dot(
        left_block.reshape(height * width_block, height),
        vector.reshape(height, -1),
        preferred_element_type=jnp.float32,
    )


def couple_terms(mixed_terms, mpo_block, height, levels):
    width_block = mpo_block.shape[0]
    shaped = mixed_terms.astype(jnp.bfloat16).reshape(height, width_block, levels, height)
    return jnp.einsum(
        "vust,avtb->asub", mpo_block, shaped, preferred_element_type=jnp.float32
    ).astype(jnp.bfloat16)


def image_rows(coupled, right_block, row_count):
    height, levels, width_block, _ = coupled.shape
    flat_right = right_block.reshape(height, width_block * height)
    result = lax.dot_general(
        coupled.reshape(row_count * levels, width_block * height),
        flat_right,
        (((1,), (1,)), ((), ())),
        preferred_element_type=jnp.float32,
    )
    return result.reshape(row_count, levels, height)


def ritz_pair(rayleigh, curvature, residual_size):
    middle = 0.5 * (rayleigh + curvature)
    half_gap = 0.5 * (rayleigh - curvature)
    lowest = middle - jnp.sqrt(half_gap * half_gap + residual_size * residual_size)
    offset = lowest - rayleigh
    length_value = jnp.sqrt(residual_size * residual_size + offset * offset)
    return (lowest, residual_size / length_value, offset / length_value)


def grow_left(left_block, mpo_block, new_state):
    height, width_block, levels = (left_block.shape[0], left_block.shape[1], new_state.shape[1])
    coupled = couple_terms(first_section(left_block, new_state), mpo_block, height, levels)
    grown = lax.dot_general(
        new_state.reshape(height * levels, height),
        coupled.reshape(height * levels, width_block * height),
        (((0,), (0,)), ((), ())),
        preferred_element_type=jnp.float32,
    )
    return grown.astype(jnp.bfloat16).reshape(height, width_block, height)


def body(left_env, right_env, mpo_site, start_state):
    left_block = left_env[0]
    mpo_block = mpo_site[0]
    height, width_block, levels = (left_block.shape[0], left_block.shape[1], start_state.shape[2])
    entries = height * levels * height
    share_rows = height // lax.axis_size("bond")
    offset_rows = lax.axis_index("bond") * share_rows
    begin_vec = start_state[0].astype(jnp.float32)
    first_basis = begin_vec / jnp.sqrt(jnp.sum(begin_vec * begin_vec) / entries + epsilon)
    first_coupled = couple_terms(
        first_section(left_block, first_basis.astype(jnp.bfloat16)), mpo_block, height, levels
    )
    right_block = shifted(right_env, "seg", -1)[0]
    first_image = lax.psum(image_rows(first_coupled, right_block, height), "bond")
    rayleigh = jnp.sum(first_basis * first_image) / entries
    residual = first_image - rayleigh * first_basis
    residual_size = jnp.sqrt(jnp.sum(residual * residual) / entries + epsilon)
    second_basis = residual / residual_size
    second_coupled = couple_terms(
        first_section(left_block, second_basis.astype(jnp.bfloat16)), mpo_block, height, levels
    )
    second_image = lax.psum(image_rows(second_coupled, right_block, height), "bond")
    curvature = jnp.sum(second_basis * second_image) / entries
    lowest, first_weight, second_weight = ritz_pair(rayleigh, curvature, residual_size)
    new_state = (first_weight * first_basis + second_weight * second_basis).astype(jnp.bfloat16)
    image_share = lax.dynamic_slice_in_dim(second_image, offset_rows, share_rows, 0)
    new_left = grow_left(left_block, mpo_block, new_state)
    return (new_state[None], new_left[None], jnp.reshape(lowest, (1,)), image_share[None])


def solution(mesh):
    in_specs = (
        P("seg", None, "bond", None),
        P("seg", None, "bond", None),
        P("seg", "bond", None, None, None),
        P("seg", None, None, None),
    )
    out_specs = (
        P("seg", None, None, None),
        P("seg", None, "bond", None),
        P("seg"),
        P("seg", "bond", None, None),
    )
    return jax.shard_map(body, mesh=mesh, in_specs=in_specs, out_specs=out_specs, check_vma=False)
```

profile of v0, /device:TPU:6, one launch (start us, length us, event | category | flops | bytes accessed | tf_op | source)
XLA Modules:
  0.0 417.4 jit_solution(12087728143959853804)
XLA Ops:
  7.2 0.0 copy-start
  7.2 0.0 all-reduce.3.cloned.1.call-start
  7.2 12.6 %collective-permute-start = (bf16[1,128,8,128]{3,2,1,0:T(8,128)(2,1)}, bf16[1,128,8,128]{3,2,1,0:T(8,128)(2,1)}, u32[]{:S(2)}, u32[]{:S(2)}) collective-permute-start(bf16[1,128,8,128]{3,2,1,0:T(8,128)(2,1)} %param.5), channel_id=1, source_target_pairs={{0,496},{16,0},{32,16},{48,32},{64,48},{80,64},{96,80},{112,96},{1... | collective-permute-start | bytes 786440 | tf_op jit(solution)/shard_map/ppermute | solution.py:12
  19.8 1.7 fusion.25
  22.2 1.0 fusion.39
  23.2 0.2 copy.17
  23.4 0.0 copy-done
  23.4 0.7 convert_bitcast_fusion.2
  24.1 0.0 copy-start.2
  24.1 2.6 copy.18
  26.7 0.0 copy-done.2
  26.7 3.6 fusion.5
  30.3 3.3 copy.21
  33.6 0.0 copy-start.1
  33.7 0.0 collective-permute-done
  33.7 1.1 reshape.58
  34.8 1.6 fusion.41
  36.3 0.0 all-reduce.3.cloned.1.call-update
  36.4 0.0 all-reduce.5.cloned.1.call-start
  36.4 170.5 %all-reduce.3.cloned.1.call-done = f32[128,8,128]{2,0,1:T(8,128)} async-done(((f32[128,8,128]{2,0,1:T(8,128)}), f32[128,8,128]{2,0,1:T(8,128)}) %all-reduce.3.cloned.1.call-update) | async-done | bytes 524304 | tf_op jit(solution)/shard_map/psum | solution.py:78
  206.9 0.0 copy-done.1
  206.9 1.8 fusion.26
  209.3 1.8 multiply_reduce_fusion.1
  211.8 1.2 fusion.40
  213.0 0.9 copy.23
  213.8 1.7 convert_bitcast_fusion.1
  215.5 2.6 copy.24
  218.1 3.6 fusion.8
  221.7 3.3 copy.27
  225.0 1.5 fusion.42
  226.6 0.0 all-reduce.5.cloned.1.call-update
  226.6 170.9 %all-reduce.5.cloned.1.call-done = f32[128,8,128]{2,0,1:T(8,128)} async-done(((f32[128,8,128]{2,0,1:T(8,128)}), f32[128,8,128]{2,0,1:T(8,128)}) %all-reduce.5.cloned.1.call-update) | async-done | bytes 524304 | tf_op jit(solution)/shard_map/psum | solution.py:86
  397.5 1.8 multiply_reduce_fusion
  400.1 0.1 fusion.29
  400.2 0.2 copy.30
  400.4 0.7 convert_bitcast_fusion
  401.1 2.6 copy.31
  403.7 2.7 fusion.20
  406.4 0.8 copy.53
  407.2 0.9 copy.35
  408.1 0.8 constant_dynamic-slice_fusion
  408.8 0.6 copy.97
Async XLA Ops:
  7.2 16.2 %copy-start = (bf16[1,128,8,128]{3,2,1,0:T(8,128)(2,1)S(1)}, bf16[1,128,8,128]{3,2,1,0:T(8,128)(2,1)}, u32[]{:S(2)}) copy-start(bf16[1,128,8,128]{3,2,1,0:T(8,128)(2,1)} %param.4) | copy-start | bytes 786436
  7.2 199.7 %all-reduce.3.cloned.1.call-start = ((), (), s32[]{:S(2)}) async-start(), calls=%async_computation | async-start | bytes 1048576 | tf_op jit(solution)/shard_map/psum | solution.py:78
  7.2 26.4 %collective-permute-start = (bf16[1,128,8,128]{3,2,1,0:T(8,128)(2,1)}, bf16[1,128,8,128]{3,2,1,0:T(8,128)(2,1)}, u32[]{:S(2)}, u32[]{:S(2)}) collective-permute-start(bf16[1,128,8,128]{3,2,1,0:T(8,128)(2,1)} %param.5), channel_id=1, source_target_pairs={{0,496},{16,0},{32,16},{48,32},{64,48},{80,64},{96,80},{112,96},{1... | collective-permute-start | bytes 786440 | tf_op jit(solution)/shard_map/ppermute | solution.py:12
  24.1 2.6 copy-start.2
  33.6 173.3 %copy-start.1 = (bf16[1,128,8,128]{3,2,1,0:T(8,128)(2,1)S(1)}, bf16[1,128,8,128]{3,2,1,0:T(8,128)(2,1)}, u32[]{:S(2)}) copy-start(bf16[1,128,8,128]{3,2,1,0:T(8,128)(2,1)} %param.7) | copy-start | bytes 786436
  36.4 361.1 %all-reduce.5.cloned.1.call-start = ((), (), s32[]{:S(2)}) async-start(), calls=%async_computation.1 | async-start | bytes 1048576 | tf_op jit(solution)/shard_map/psum | solution.py:86
Sparse Core Ops, SparseCore 0:
  36.5 170.3 all-reduce.2
  226.7 170.7 all-reduce.4
where the time goes:
time: 418 us; the launch traced here: 417 us
  waiting for transfers between devices  341 us (82%)
  local copies, waits for them, and re-layouts  19.7 us (5%)
  between operations  18.2 us (4%)
  matrix products  16.1 us (4%)
  starting transfers between devices  12.7 us (3%)
  other arithmetic  9.33 us (2%)
    psum x1, waiting for transfers between devices, body(): lax.psum(image_rows(second_coupled, right_block, height), 'bond')  171 us
    psum x1, waiting for transfers between devices, body(): lax.psum(image_rows(first_coupled, right_block, height), 'bond')  170 us
    ppermute x1, starting transfers between devices, shifted(): return lax.ppermute(value, axis, pairs)  12.6 us
  transfers between devices with their start and end apart: 3, of which 2 were waited for; matrix products, arithmetic and copies ran while one was open for 3% of the time, Pallas kernels for 0%

commit v1 on v0

v1 whole, which is shorter than its diff:
```python
import jax
import jax.numpy as jnp
from jax import lax
from jax.experimental import pallas as pl
from jax.experimental.pallas import tpu as pltpu
from jax.sharding import PartitionSpec as P

epsilon = 1e-06
MESH = pl.DeviceIdType.MESH
f32, bf16 = jnp.float32, jnp.bfloat16


def total(value):
    return jnp.sum(jnp.sum(value, axis=1, keepdims=True), axis=0, keepdims=True)


def kernel(segs, bonds, left_hbm, right_hbm, mpo_hbm, start_hbm,
           state_ref, grown_ref, energy_ref, image_ref,
           left, right, mpo, start, spread, wide, stacked, coupler,
           coupled_1, coupled_2, partial, start_t, resid_t,
           send_1, send_2, recv_1, recv_2, resid, scal_send, scal_recv,
           grown_11, grown_x, grown_22,
           local_sem, ring_sem, block_send, block_recv, scal_send_sem, scal_recv_sem):
    seg, me = lax.axis_index("seg"), lax.axis_index("bond")
    before, after = lax.rem(seg + segs - 1, segs), lax.rem(seg + 1, segs)
    rows = partial.shape[0] // bonds
    entries = partial.shape[0] * partial.shape[1]
    peers = [lax.rem(me + step, bonds) for step in range(1, bonds)]

    barrier = pltpu.get_barrier_semaphore()
    pl.semaphore_signal(barrier, inc=1, device_id=(before, me), device_id_type=MESH)
    pl.semaphore_signal(barrier, inc=1, device_id=(after, me), device_id_type=MESH)
    for peer in peers:
        pl.semaphore_signal(barrier, inc=1, device_id=(seg, peer), device_id_type=MESH)

    loads = [
        pltpu.make_async_copy(source, target, local_sem.at[place])
        for place, (source, target) in enumerate(((start_hbm, start), (left_hbm, left), (mpo_hbm, mpo)))
    ]
    for load in loads:
        load.start()
    pl.semaphore_wait(barrier, bonds + 1)

    ring = pltpu.make_async_remote_copy(
        src_ref=right_hbm, dst_ref=right, send_sem=ring_sem.at[0], recv_sem=ring_sem.at[1],
        device_id=(before, me), device_id_type=MESH)
    ring.start()

    def level_major(source):
        spread[...] = source[...].astype(f32)
        for t in range(8):
            wide[:, t * 128:(t + 1) * 128] = spread[pl.ds(t, 128, stride=8), :].astype(bf16)

    def couple(target):
        def step(i, carry):
            mixed = jnp.dot(left[pl.ds(i * 256, 256), :], wide[...], preferred_element_type=f32)
            shaped = jnp.stack([mixed[:, t * 128:(t + 1) * 128].reshape(32, 8, 128) for t in range(8)], axis=1)
            shaped = shaped.reshape(2048, 128).astype(bf16)
            for g in range(4):
                pair = jnp.concatenate(
                    [shaped[g * 512:g * 512 + 256], shaped[g * 512 + 256:g * 512 + 512]], axis=1)
                out = jnp.dot(coupler[...], pair, preferred_element_type=f32)
                for h in range(2):
                    half = out[:, h * 128:(h + 1) * 128].reshape(4, 8, 8, 128)
                    for u in range(8):
                        target[pl.ds(i * 256 + g * 64 + h * 32, 32), u * 128:(u + 1) * 128] = (
                            half[:, u].reshape(32, 128).astype(bf16))
            return carry
        lax.fori_loop(0, 4, step, 0)

    def image(source, vector, sent, scale):
        def step(i, carry):
            span = pl.ds(i * 256, 256)
            part = jnp.dot(source[span, :], stacked[...], preferred_element_type=f32)
            dots = jnp.sum((part * vector[span, :].astype(f32)).reshape(32, 8, 128), axis=0)
            if scale is not None:
                part = part * scale
            partial[span, :] = part
            sent[span, :] = part.astype(bf16)
            return carry + dots
        return total(lax.fori_loop(0, 4, step, jnp.zeros((8, 128), f32)))

    def grow(pairs, target):
        for u in range(0, 8, 2):
            lanes = slice(u * 128, (u + 2) * 128)
            value = None
            for transposed, source in pairs:
                term = jnp.dot(transposed[...], source[:, lanes], preferred_element_type=f32)
                value = term if value is None else value + term
            target[pl.ds(u, 128, stride=8), :] = value[:, :128]
            target[pl.ds(u + 1, 128, stride=8), :] = value[:, 128:]

    def scalar_round(phase, value):
        scal_send[phase] = jnp.broadcast_to(value, (8, 128))
        copies = []
        for step, peer in enumerate(peers):
            copies.append(pltpu.make_async_remote_copy(
                src_ref=scal_send.at[phase], dst_ref=scal_recv.at[phase, me],
                send_sem=scal_send_sem.at[phase, step], recv_sem=scal_recv_sem.at[phase, step],
                device_id=(seg, peer), device_id_type=MESH))
            copies[-1].start()
        scal_recv[phase, me] = scal_send[phase]
        return copies

    def scalar_sum(phase, copies):
        for copy in copies:
            copy.wait()
        return jnp.sum(scal_recv[phase], axis=0)[:1, :1]

    def scatter_round(phase, source, target):
        copies = []
        for step, peer in enumerate(peers):
            copies.append(pltpu.make_async_remote_copy(
                src_ref=source.at[pl.ds(pl.multiple_of(peer * rows, rows), rows), :], dst_ref=target.at[step],
                send_sem=block_send.at[phase, step], recv_sem=block_recv.at[phase, step],
                device_id=(seg, peer), device_id_type=MESH))
            copies[-1].start()
        return copies

    own = pl.ds(pl.multiple_of(me * rows, rows), rows)

    def scatter_sum(copies, target):
        value = partial[own, :]
        for step, copy in enumerate(copies):
            copy.wait()
            value = value + target[step].astype(f32)
        return value

    loads[0].wait()
    level_major(start)
    norm = total(jnp.sum((spread[...] * spread[...]).reshape(-1, 8, 128), axis=0))
    inverse = 1.0 / jnp.sqrt(norm / entries + epsilon)
    loads[2].wait()
    spot = lax.broadcasted_iota(jnp.int32, (8, 256), 0)
    lane = lax.broadcasted_iota(jnp.int32, (8, 256), 1)
    compact = jnp.zeros((64, 256), f32)
    for w in range(8):
        chosen = jnp.where(lax.rem(lane, 64) == spot * 8 + w, 1.0, 0.0).astype(f32)
        compact = compact + jnp.dot(
            mpo[w].astype(f32).reshape(64, 8), chosen, preferred_element_type=f32)
    tall = jnp.concatenate([compact] * 4, axis=0)
    row_group = lax.broadcasted_iota(jnp.int32, (256, 256), 0) // 64
    lane_group = lax.broadcasted_iota(jnp.int32, (256, 256), 1) // 64
    coupler[...] = jnp.where(row_group == lane_group, tall, 0.0).astype(bf16)
    loads[1].wait()
    couple(coupled_1)
    start_t[...] = jnp.transpose(start[...])

    ring.wait()
    spread[...] = right[...].astype(f32)
    for u in range(8):
        stacked[u * 128:(u + 1) * 128, :] = spread[pl.ds(u, 128, stride=8), :].astype(bf16)
    ray_copies = scalar_round(0, image(coupled_1, start, send_1, None))
    copies = scatter_round(0, send_1, recv_1)
    grow([(start_t, coupled_1)], grown_11)
    rayleigh = scalar_sum(0, ray_copies) * (inverse * inverse / entries)
    image_1 = scatter_sum(copies, recv_1)
    block = inverse * image_1 - (rayleigh * inverse) * start[own, :].astype(f32)
    resid[own, :] = block.astype(bf16)
    size_copies = scalar_round(1, total(block * block))
    copies = []
    for step, peer in enumerate(peers):
        copies.append(pltpu.make_async_remote_copy(
            src_ref=resid.at[own, :], dst_ref=resid.at[own, :],
            send_sem=block_send.at[1, step], recv_sem=block_recv.at[1, step],
            device_id=(seg, peer), device_id_type=MESH))
        copies[-1].start()
    for copy in copies:
        copy.wait()

    level_major(resid)
    couple(coupled_2)
    size = jnp.sqrt(scalar_sum(1, size_copies) / entries + epsilon)
    curve = image(coupled_2, resid, send_2, 1.0 / size)
    curve_copies = scalar_round(2, curve)
    copies = scatter_round(2, send_2, recv_2)
    resid_t[...] = jnp.transpose(resid[...])
    grow([(start_t, coupled_2), (resid_t, coupled_1)], grown_x)
    grow([(resid_t, coupled_2)], grown_22)
    curvature = scalar_sum(2, curve_copies) / (size * size * entries)
    middle = 0.5 * (rayleigh + curvature)
    half_gap = 0.5 * (rayleigh - curvature)
    lowest = middle - jnp.sqrt(half_gap * half_gap + size * size)
    offset = lowest - rayleigh
    length = jnp.sqrt(size * size + offset * offset)
    first = size / length * inverse
    second = offset / length / size
    energy_ref[0] = lowest[0, 0]
    state_ref[...] = (first * start[...].astype(f32) + second * resid[...].astype(f32)).astype(bf16)
    grown_ref[...] = (first * first * grown_11[...] + first * second * grown_x[...]
                      + second * second * grown_22[...]).astype(bf16)
    image_ref[...] = scatter_sum(copies, recv_2)


def solution(mesh):
    segs, bonds = mesh.shape["seg"], mesh.shape["bond"]

    def body(left_env, right_env, mpo_site, start_state):
        big, half = (1024, 128), (1024 // bonds, 128)
        anywhere = pl.BlockSpec(memory_space=pl.ANY)
        vmem = pl.BlockSpec(memory_space=pltpu.VMEM)
        state, grown, energy, image = pl.pallas_call(
            lambda *refs: kernel(segs, bonds, *refs),
            out_shape=(
                jax.ShapeDtypeStruct(big, bf16),
                jax.ShapeDtypeStruct(big, bf16),
                jax.ShapeDtypeStruct((1,), f32),
                jax.ShapeDtypeStruct(half, f32),
            ),
            in_specs=[anywhere] * 4,
            out_specs=(vmem, vmem, pl.BlockSpec(memory_space=pltpu.SMEM), vmem),
            scratch_shapes=[
                pltpu.VMEM(big, bf16),
                pltpu.VMEM(big, bf16),
                pltpu.VMEM((8, 8, 8, 8), bf16),
                pltpu.VMEM(big, bf16),
                pltpu.VMEM(big, f32),
                pltpu.VMEM((128, 1024), bf16),
                pltpu.VMEM(big, bf16),
                pltpu.VMEM((256, 256), bf16),
                pltpu.VMEM((1024, 1024), bf16),
                pltpu.VMEM((1024, 1024), bf16),
                pltpu.VMEM(big, f32),
                pltpu.VMEM((128, 1024), bf16),
                pltpu.VMEM((128, 1024), bf16),
                pltpu.VMEM(big, bf16),
                pltpu.VMEM(big, bf16),
                pltpu.VMEM((bonds - 1,) + half, bf16),
                pltpu.VMEM((bonds - 1,) + half, bf16),
                pltpu.VMEM(big, bf16),
                pltpu.VMEM((3, 8, 128), f32),
                pltpu.VMEM((3, bonds, 8, 128), f32),
                pltpu.VMEM(big, f32),
                pltpu.VMEM(big, f32),
                pltpu.VMEM(big, f32),
                pltpu.SemaphoreType.DMA((3,)),
                pltpu.SemaphoreType.DMA((2,)),
                pltpu.SemaphoreType.DMA((3, bonds - 1)),
                pltpu.SemaphoreType.DMA((3, bonds - 1)),
                pltpu.SemaphoreType.DMA((3, bonds - 1)),
                pltpu.SemaphoreType.DMA((3, bonds - 1)),
            ],
            compiler_params=pltpu.CompilerParams(
                collective_id=0, has_side_effects=True, vmem_limit_bytes=60 * 1024 * 1024),
            name="ritz_step",
        )(left_env.reshape(big), right_env.reshape(big), mpo_site[0], start_state.reshape(big))
        return (
            state.reshape(1, 128, 8, 128),
            grown.reshape(1, 128, 8, 128),
            energy,
            image.reshape(1, 1024 // bonds // 8, 8, 128),
        )

    in_specs = (
        P("seg", None, "bond", None),
        P("seg", None, "bond", None),
        P("seg", "bond", None, None, None),
        P("seg", None, None, None),
    )
    out_specs = (
        P("seg", None, None, None),
        P("seg", None, "bond", None),
        P("seg"),
        P("seg", "bond", None, None),
    )
    return jax.shard_map(body, mesh=mesh, in_specs=in_specs, out_specs=out_specs, check_vma=False)
```

time: 418 us -> 65.4 us (0.16)
  the two profiles are of different devices: /device:TPU:6 before, /device:TPU:32 now
where the time goes in v1:
time: 65.4 us; the launch traced here: 65.3 us
  Pallas kernels  59.8 us (91%)
  local copies, waits for them, and re-layouts  3.04 us (5%)
  between operations  2.46 us (4%)
    pallas_call x1, Pallas kernels, body(): pl.pallas_call(lambda *refs: kernel(segs, bonds, *refs), out_shape=(jax.S...  59.8 us
    unnamed x7, local copies, waits for them, and re-layouts  3.04 us

profile of v1, /device:TPU:32, one launch (start us, length us, event | category | flops | bytes accessed | tf_op | source)
XLA Modules:
  0.0 65.3 jit_solution(4560946500111675282)
XLA Ops:
  0.6 59.8 %ritz_step.1 = (bf16[1024,128]{1,0:T(8,128)(2,1)}, bf16[1024,128]{1,0:T(8,128)(2,1)}, f32[1]{0:T(128)}, f32[64,128]{1,0:T(8,128)}) custom-call(bf16[1024,128]{1,0:T(8,128)(2,1)} %bitcast.7, bf16[1024,128]{1,0:T(8,128)(2,1)} %bitcast.8, bf16[8,8,8,8]{3,2,1,0:T(8,128)(2,1)} %bitcast.12, bf16[1024,128]{1,0:T(8,128)(2,1)} %bitcast.9), custom_call_target="tpu_custom_call" | custom-call | tf_op jit(solution)/shard_map/ritz_step/pallas_call | solution.py:202
  60.4 0.0 copy-start
  60.4 1.7 %copy.12 = bf16[1,128,8,128]{3,2,1,0:T(8,128)(2,1)} copy(bf16[1,128,8,128]{3,2,1,0:T(8,128)(2,1)} %bitcast.11) | data formatting | bytes 524288
  62.1 0.0 copy-done
  62.1 0.0 copy-start.1
  62.1 0.7 %copy.13 = bf16[1,128,8,128]{3,2,1,0:T(8,128)(2,1)} copy(bf16[1,128,8,128]{3,2,1,0:T(8,128)(2,1)S(1)} %bitcast.10) | data formatting | bytes 524288
  63.5 0.0 copy-done.1
  63.5 0.6 copy.15
Async XLA Ops:
  60.4 1.7 %copy-start = (bf16[1024,128]{1,0:T(8,128)(2,1)S(1)}, bf16[1024,128]{1,0:T(8,128)(2,1)}, u32[]{:S(2)}) copy-start(bf16[1024,128]{1,0:T(8,128)(2,1)} %get-tuple-element.9) | copy-start | bytes 786436
  62.1 1.4 %copy-start.1 = (f32[64,128]{1,0:T(8,128)S(1)}, f32[64,128]{1,0:T(8,128)}, u32[]{:S(2)}) copy-start(f32[64,128]{1,0:T(8,128)} %get-tuple-element.11) | copy-start | bytes 98308

commit v2 on v1

v2 whole, which is shorter than its diff:
```python
import jax
import jax.numpy as jnp
from jax import lax
from jax.experimental import pallas as pl
from jax.experimental.pallas import tpu as pltpu
from jax.sharding import PartitionSpec as P

epsilon = 1e-06
MESH = pl.DeviceIdType.MESH
f32, bf16 = jnp.float32, jnp.bfloat16
ROW, SIDE = 4, 4
CHUNKS = 4


def total(value):
    return jnp.sum(jnp.sum(value, axis=1, keepdims=True), axis=0, keepdims=True)


def kernel(segs, bonds, left_hbm, right_hbm, mpo_hbm, start_hbm,
           state_ref, grown_ref, energy_ref, image_ref,
           left, right, mpo, start, spread, wide, stacked, coupler, pack_send, pack_recv, edge_send, edge_recv,
           coupled_1, coupled_2, partial, start_t, resid_t,
           send_1, send_2, recv_1, recv_2, resid, scal_send, scal_recv,
           grown_11, grown_x, grown_22,
           local_sem, ring_send, ring_recv, block_send, block_recv, scal_send_sem, scal_recv_sem):
    seg, me = lax.axis_index("seg"), lax.axis_index("bond")
    before, after = lax.rem(seg + segs - 1, segs), lax.rem(seg + 1, segs)
    rows = partial.shape[0] // bonds
    entries = partial.shape[0] * partial.shape[1]
    row, place = me // SIDE, lax.rem(me, SIDE)
    row_order = [3 - row, lax.rem(row + 2, ROW), row + 1 - 2 * lax.rem(row, 2), row]
    peers = []
    for k, other in enumerate(row_order):
        for j in (2, 1, 3, 0):
            if k < 3 or j:
                peers.append(other * SIDE + lax.rem(place + j, SIDE))
    by_row = [range(0, 4), range(4, 8), range(8, 12), range(12, 15)]

    barrier = pltpu.get_barrier_semaphore()
    pl.semaphore_signal(barrier, inc=1, device_id=(before, me), device_id_type=MESH)
    pl.semaphore_signal(barrier, inc=1, device_id=(after, me), device_id_type=MESH)
    for peer in peers:
        pl.semaphore_signal(barrier, inc=1, device_id=(seg, peer), device_id_type=MESH)

    loads = [
        pltpu.make_async_copy(source, target, local_sem.at[spot])
        for spot, (source, target) in enumerate(
            ((right_hbm, right), (start_hbm, start), (left_hbm, left), (mpo_hbm, mpo)))
    ]
    for load in loads:
        load.start()

    up = lax.broadcasted_iota(jnp.int32, (64, 128), 0)
    lane = lax.broadcasted_iota(jnp.int32, (64, 128), 1)
    keep = jnp.where(lane < 64, jnp.where(lane <= up, 1, 0), jnp.where(lane - 64 > up, 1, 0)) == 1
    near, far = lane == up, lane == up + 64
    loads[0].wait()
    spread[...] = right[...].astype(f32)
    for u in range(8):
        low = spread[pl.ds(u, 64, stride=8), :]
        high = spread[pl.ds(512 + u, 64, stride=8), :]
        pack_send[u] = jnp.where(keep, low, high).astype(bf16)
        edge_send[u:u + 1, :] = jnp.sum(
            jnp.where(far, low, 0.0) + jnp.where(near, high, 0.0), axis=0, keepdims=True)
    pl.semaphore_wait(barrier, bonds + 1)

    share = 8 // CHUNKS
    ring = [pltpu.make_async_remote_copy(
        src_ref=edge_send, dst_ref=edge_recv, send_sem=ring_send.at[CHUNKS], recv_sem=ring_recv.at[CHUNKS],
        device_id=(before, me), device_id_type=MESH)]
    for c in range(CHUNKS):
        part = pl.ds(c * share, share)
        ring.append(pltpu.make_async_remote_copy(
            src_ref=pack_send.at[part], dst_ref=pack_recv.at[part],
            send_sem=ring_send.at[c], recv_sem=ring_recv.at[c],
            device_id=(before, me), device_id_type=MESH))
    for copy in ring:
        copy.start()

    def unpack(u):
        half = pack_recv[u].astype(f32)
        turned = jnp.transpose(jnp.concatenate([half, half], axis=0))
        edge = jnp.broadcast_to(edge_recv[u:u + 1, :], (64, 128))
        top = jnp.where(far, edge, jnp.where(keep, half, turned[:64]))
        low = jnp.where(near, edge, jnp.where(keep, turned[64:], half))
        stacked[u * 128:u * 128 + 64, :] = top.astype(bf16)
        stacked[u * 128 + 64:u * 128 + 128, :] = low.astype(bf16)

    def couple(target):
        def step(i, carry):
            mixed = jnp.dot(left[pl.ds(i * 256, 256), :], wide[...], preferred_element_type=f32)
            shaped = jnp.stack([mixed[:, t * 128:(t + 1) * 128].reshape(32, 8, 128) for t in range(8)], axis=1)
            shaped = shaped.reshape(2048, 128).astype(bf16)
            for g in range(4):
                pair = jnp.concatenate(
                    [shaped[g * 512:g * 512 + 256], shaped[g * 512 + 256:g * 512 + 512]], axis=1)
                out = jnp.dot(coupler[...], pair, preferred_element_type=f32)
                for h in range(2):
                    half = out[:, h * 128:(h + 1) * 128].reshape(4, 8, 8, 128)
                    for u in range(8):
                        target[pl.ds(i * 256 + g * 64 + h * 32, 32), u * 128:(u + 1) * 128] = (
                            half[:, u].reshape(32, 128).astype(bf16))
            return carry
        lax.fori_loop(0, 4, step, 0)

    def scatter_copy(phase, step, source, target):
        peer = peers[step]
        return pltpu.make_async_remote_copy(
            src_ref=source.at[pl.ds(pl.multiple_of(peer * rows, rows), rows), :], dst_ref=target.at[step],
            send_sem=block_send.at[phase, step], recv_sem=block_recv.at[phase, step],
            device_id=(seg, peer), device_id_type=MESH)

    def image(source, vector, sent, target, phase, scale, first, more):
        lanes = slice(first, 1024)
        dots = jnp.zeros((8, 128), f32)
        copies = []
        for k in range(4):
            span = pl.ds(pl.multiple_of(row_order[k] * 256, 256), 256)
            part = jnp.dot(source[span, lanes], stacked[lanes, :], preferred_element_type=f32)
            if more:
                part = part + partial[span, :]
            dots = dots + jnp.sum((part * vector[span, :].astype(f32)).reshape(32, 8, 128), axis=0)
            if scale is not None:
                part = part * scale
            partial[span, :] = part
            sent[span, :] = part.astype(bf16)
            for step in by_row[k]:
                copies.append(scatter_copy(phase, step, sent, target))
                copies[-1].start()
        return total(dots), copies

    def grow(pairs, target):
        for u in range(0, 8, 2):
            lanes = slice(u * 128, (u + 2) * 128)
            value = None
            for transposed, source in pairs:
                term = jnp.dot(transposed[...], source[:, lanes], preferred_element_type=f32)
                value = term if value is None else value + term
            target[pl.ds(u, 128, stride=8), :] = value[:, :128]
            target[pl.ds(u + 1, 128, stride=8), :] = value[:, 128:]

    def scalar_round(phase, value):
        scal_send[phase] = jnp.broadcast_to(value, (8, 128))
        copies = []
        for step, peer in enumerate(peers):
            copies.append(pltpu.make_async_remote_copy(
                src_ref=scal_send.at[phase], dst_ref=scal_recv.at[phase, me],
                send_sem=scal_send_sem.at[phase, step], recv_sem=scal_recv_sem.at[phase, step],
                device_id=(seg, peer), device_id_type=MESH))
            copies[-1].start()
        scal_recv[phase, me] = scal_send[phase]
        return copies

    def scalar_sum(phase, copies):
        for copy in copies:
            copy.wait()
        return jnp.sum(scal_recv[phase], axis=0)[:1, :1]

    own = pl.ds(pl.multiple_of(me * rows, rows), rows)

    def scatter_sum(copies, target):
        value = partial[own, :]
        for step in reversed(range(len(copies))):
            copies[step].wait()
            value = value + target[step].astype(f32)
        return value

    loads[1].wait()
    spread[...] = start[...].astype(f32)
    for t in range(8):
        wide[:, t * 128:(t + 1) * 128] = spread[pl.ds(t, 128, stride=8), :].astype(bf16)
    norm = total(jnp.sum((spread[...] * spread[...]).reshape(-1, 8, 128), axis=0))
    inverse = 1.0 / jnp.sqrt(norm / entries + epsilon)
    loads[3].wait()
    spot = lax.broadcasted_iota(jnp.int32, (8, 256), 0)
    wide_lane = lax.broadcasted_iota(jnp.int32, (8, 256), 1)
    compact = jnp.zeros((64, 256), f32)
    for w in range(8):
        chosen = jnp.where(lax.rem(wide_lane, 64) == spot * 8 + w, 1.0, 0.0).astype(f32)
        compact = compact + jnp.dot(
            mpo[w].astype(f32).reshape(64, 8), chosen, preferred_element_type=f32)
    tall = jnp.concatenate([compact] * 4, axis=0)
    row_group = lax.broadcasted_iota(jnp.int32, (256, 256), 0) // 64
    lane_group = lax.broadcasted_iota(jnp.int32, (256, 256), 1) // 64
    coupler[...] = jnp.where(row_group == lane_group, tall, 0.0).astype(bf16)
    loads[2].wait()
    couple(coupled_1)
    start_t[...] = jnp.transpose(start[...])

    ring[0].wait_recv()
    for c in range(CHUNKS):
        ring[1 + c].wait_recv()
        for u in range(c * share, (c + 1) * share):
            unpack(u)
        if c < CHUNKS - 1:
            def add(i, carry, c=c):
                span, lanes = pl.ds(i * 256, 256), slice(c * share * 128, (c + 1) * share * 128)
                part = jnp.dot(coupled_1[span, lanes], stacked[lanes, :], preferred_element_type=f32)
                partial[span, :] = part if c == 0 else partial[span, :] + part
                return carry
            lax.fori_loop(0, 4, add, 0)
    ray, copies = image(coupled_1, start, send_1, recv_1, 0, None, (CHUNKS - 1) * share * 128, True)
    ray_copies = scalar_round(0, ray)
    grow([(start_t, coupled_1)], grown_11)
    rayleigh = scalar_sum(0, ray_copies) * (inverse * inverse / entries)
    image_1 = scatter_sum(copies, recv_1)
    block = inverse * image_1 - (rayleigh * inverse) * start[own, :].astype(f32)
    resid[own, :] = block.astype(bf16)
    copies = []
    for step, peer in enumerate(peers):
        copies.append(pltpu.make_async_remote_copy(
            src_ref=resid.at[own, :], dst_ref=resid.at[own, :],
            send_sem=block_send.at[1, step], recv_sem=block_recv.at[1, step],
            device_id=(seg, peer), device_id_type=MESH))
        copies[-1].start()
    size_copies = scalar_round(1, total(block * block))

    for k in (3, 2, 1, 0):
        for step in by_row[k]:
            copies[step].wait()
        span = pl.ds(pl.multiple_of(row_order[k] * 256, 256), 256)
        spread[span, :] = resid[span, :].astype(f32)
        for t in range(8):
            wide[pl.ds(pl.multiple_of(row_order[k] * 32, 32), 32), t * 128:(t + 1) * 128] = (
                spread[pl.ds(row_order[k] * 256 + t, 32, stride=8), :].astype(bf16))
    couple(coupled_2)
    size = jnp.sqrt(scalar_sum(1, size_copies) / entries + epsilon)
    curve, copies = image(coupled_2, resid, send_2, recv_2, 2, 1.0 / size, 0, False)
    curve_copies = scalar_round(2, curve)
    resid_t[...] = jnp.transpose(resid[...])
    grow([(start_t, coupled_2), (resid_t, coupled_1)], grown_x)
    grow([(resid_t, coupled_2)], grown_22)
    curvature = scalar_sum(2, curve_copies) / (size * size * entries)
    middle = 0.5 * (rayleigh + curvature)
    half_gap = 0.5 * (rayleigh - curvature)
    lowest = middle - jnp.sqrt(half_gap * half_gap + size * size)
    offset = lowest - rayleigh
    length = jnp.sqrt(size * size + offset * offset)
    first = size / length * inverse
    second = offset / length / size
    energy_ref[...] = jnp.broadcast_to(lowest, (8, 128))
    state_ref[...] = (first * start[...].astype(f32) + second * resid[...].astype(f32)).astype(bf16)
    grown_ref[...] = (first * first * grown_11[...] + first * second * grown_x[...]
                      + second * second * grown_22[...]).astype(bf16)
    for copy in ring:
        copy.wait_send()
    image_ref[...] = scatter_sum(copies, recv_2)


def write_out(state, grown, energy, image, state_out, grown_out, energy_out, image_out, sems):
    copies = [
        pltpu.make_async_copy(source, target, sems.at[spot])
        for spot, (source, target) in enumerate(((state, state_out), (grown, grown_out), (image, image_out)))
    ]
    for copy in copies:
        copy.start()
    energy_out[0] = energy[0, 0]
    for copy in copies:
        copy.wait()


def solution(mesh):
    segs, bonds = mesh.shape["seg"], mesh.shape["bond"]

    def body(left_env, right_env, mpo_site, start_state):
        big, half = (1024, 128), (1024 // bonds, 128)
        anywhere = pl.BlockSpec(memory_space=pl.ANY)
        vmem = pl.BlockSpec(memory_space=pltpu.VMEM)
        results = pl.pallas_call(
            lambda *refs: kernel(segs, bonds, *refs),
            out_shape=(pltpu.VMEM(big, bf16), pltpu.VMEM(big, bf16), pltpu.VMEM((8, 128), f32), pltpu.VMEM(half, f32)),
            in_specs=[pl.BlockSpec(memory_space=pltpu.HBM)] * 4,
            out_specs=(vmem,) * 4,
            scratch_shapes=[
                pltpu.VMEM(big, bf16),
                pltpu.VMEM(big, bf16),
                pltpu.VMEM((8, 8, 8, 8), bf16),
                pltpu.VMEM(big, bf16),
                pltpu.VMEM(big, f32),
                pltpu.VMEM((128, 1024), bf16),
                pltpu.VMEM(big, bf16),
                pltpu.VMEM((256, 256), bf16),
                pltpu.VMEM((8, 64, 128), bf16),
                pltpu.VMEM((8, 64, 128), bf16),
                pltpu.VMEM((8, 128), f32),
                pltpu.VMEM((8, 128), f32),
                pltpu.VMEM((1024, 1024), bf16),
                pltpu.VMEM((1024, 1024), bf16),
                pltpu.VMEM(big, f32),
                pltpu.VMEM((128, 1024), bf16),
                pltpu.VMEM((128, 1024), bf16),
                pltpu.VMEM(big, bf16),
                pltpu.VMEM(big, bf16),
                pltpu.VMEM((bonds - 1,) + half, bf16),
                pltpu.VMEM((bonds - 1,) + half, bf16),
                pltpu.VMEM(big, bf16),
                pltpu.VMEM((3, 8, 128), f32),
                pltpu.VMEM((3, bonds, 8, 128), f32),
                pltpu.VMEM(big, f32),
                pltpu.VMEM(big, f32),
                pltpu.VMEM(big, f32),
                pltpu.SemaphoreType.DMA((4,)),
                pltpu.SemaphoreType.DMA((CHUNKS + 1,)),
                pltpu.SemaphoreType.DMA((CHUNKS + 1,)),
                pltpu.SemaphoreType.DMA((3, bonds - 1)),
                pltpu.SemaphoreType.DMA((3, bonds - 1)),
                pltpu.SemaphoreType.DMA((3, bonds - 1)),
                pltpu.SemaphoreType.DMA((3, bonds - 1)),
            ],
            compiler_params=pltpu.CompilerParams(
                collective_id=0, has_side_effects=True, vmem_limit_bytes=32 * 1024 * 1024),
            name="ritz_step",
        )(*(pltpu.with_memory_space_constraint(x, pltpu.HBM) for x in (
            left_env.reshape(big), right_env.reshape(big), mpo_site[0], start_state.reshape(big))))
        state, grown, energy, image = pl.pallas_call(
            write_out,
            out_shape=(
                jax.ShapeDtypeStruct(big, bf16),
                jax.ShapeDtypeStruct(big, bf16),
                jax.ShapeDtypeStruct((1,), f32),
                jax.ShapeDtypeStruct(half, f32),
            ),
            in_specs=[vmem] * 4,
            out_specs=(anywhere, anywhere, pl.BlockSpec(memory_space=pltpu.SMEM), anywhere),
            scratch_shapes=[pltpu.SemaphoreType.DMA((3,))],
            compiler_params=pltpu.CompilerParams(vmem_limit_bytes=8 * 1024 * 1024),
            name="write_out",
        )(*results)
        return (
            state.reshape(1, 128, 8, 128),
            grown.reshape(1, 128, 8, 128),
            energy,
            image.reshape(1, 1024 // bonds // 8, 8, 128),
        )

    in_specs = (
        P("seg", None, "bond", None),
        P("seg", None, "bond", None),
        P("seg", "bond", None, None, None),
        P("seg", None, None, None),
    )
    out_specs = (
        P("seg", None, None, None),
        P("seg", None, "bond", None),
        P("seg"),
        P("seg", "bond", None, None),
    )
    return jax.shard_map(body, mesh=mesh, in_specs=in_specs, out_specs=out_specs, check_vma=False)
```

time: 65.4 us -> 55.9 us (0.85)
  the two profiles are of different devices: /device:TPU:32 before, /device:TPU:1 now
where the time goes in v2:
time: 55.9 us; the launch traced here: 55.8 us
  Pallas kernels  55.1 us (99%)
  between operations  0.64 us (1%)
    pallas_call x1, Pallas kernels, body(): pl.pallas_call(lambda *refs: kernel(segs, bonds, *refs), out_shape=(pltpu...  53.8 us
    pallas_call x1, Pallas kernels, body(): pl.pallas_call(write_out, out_shape=(jax.ShapeDtypeStruct(big, bf16), jax...  1.34 us

profile of v2, /device:TPU:1, one launch (start us, length us, event | category | flops | bytes accessed | tf_op | source)
XLA Modules:
  0.0 55.8 jit_solution(11765650248583268528)
XLA Ops:
  0.6 53.8 %ritz_step.1 = (bf16[1024,128]{1,0:T(8,128)(2,1)S(1)}, bf16[1024,128]{1,0:T(8,128)(2,1)S(1)}, f32[8,128]{1,0:T(8,128)S(1)}, f32[64,128]{1,0:T(8,128)S(1)}) custom-call(bf16[1024,128]{1,0:T(8,128)(2,1)} %bitcast.7, bf16[1024,128]{1,0:T(8,128)(2,1)} %bitcast.8, bf16[8,8,8,8]{3,2,1,0:T(8,128)(2,1)} %bitcast.10, bf16[1024,128]{1,0:T(8,128)(2,1)} %bitcast.9), custom_call_target="tpu_custom_call" | custom-call | tf_op jit(solution)/shard_map/ritz_step/pallas_call | solution.py:269
  54.4 1.3 %write_out.1 = (bf16[1024,128]{1,0:T(8,128)(2,1)}, bf16[1024,128]{1,0:T(8,128)(2,1)}, f32[1]{0:T(128)}, f32[64,128]{1,0:T(8,128)}) custom-call(bf16[1024,128]{1,0:T(8,128)(2,1)S(1)} %get-tuple-element.12.state, bf16[1024,128]{1,0:T(8,128)(2,1)S(1)} %get-tuple-element.13.grown, f32[8,128]{1,0:T(8,128)S(1)} %get-tuple-element.14.energy, ...), custom_call_target="tpu_custom_call" | custom-call | tf_op jit(solution)/shard_map/write_out/pallas_call | solution.py:315

commit v3 on v2

--- a/solution.py
+++ b/solution.py
@@ -20,9 +20,9 @@
            state_ref, grown_ref, energy_ref, image_ref,
            left, right, mpo, start, spread, wide, stacked, coupler, pack_send, pack_recv, edge_send, edge_recv,
            coupled_1, coupled_2, partial, start_t, resid_t,
-           send_1, send_2, recv_1, recv_2, resid, scal_send, scal_recv,
+           send_1, send_2, side_1, side_2, sums_1, sums_2, recv_1, recv_2, resid, scal_send, scal_recv,
            grown_11, grown_x, grown_22,
-           local_sem, ring_send, ring_recv, block_send, block_recv, scal_send_sem, scal_recv_sem):
+           ready, distant, local_sem, ring_send, ring_recv, block_send, block_recv, scal_send_sem, scal_recv_sem):
     seg, me = lax.axis_index("seg"), lax.axis_index("bond")
     before, after = lax.rem(seg + segs - 1, segs), lax.rem(seg + 1, segs)
     rows = partial.shape[0] // bonds
@@ -34,13 +34,24 @@
         for j in (2, 1, 3, 0):
             if k < 3 or j:
                 peers.append(other * SIDE + lax.rem(place + j, SIDE))
-    by_row = [range(0, 4), range(4, 8), range(8, 12), range(12, 15)]
-
+    pending = []
+
+    early, late = lax.rem(seg, 8) == 0, lax.rem(seg, 8) == 7
+    beside = [row * SIDE + lax.rem(place + j, SIDE) for j in range(1, SIDE)]
     barrier = pltpu.get_barrier_semaphore()
-    pl.semaphore_signal(barrier, inc=1, device_id=(before, me), device_id_type=MESH)
-    pl.semaphore_signal(barrier, inc=1, device_id=(after, me), device_id_type=MESH)
-    for peer in peers:
-        pl.semaphore_signal(barrier, inc=1, device_id=(seg, peer), device_id_type=MESH)
+
+    def enter(device, semaphore=barrier):
+        pl.semaphore_signal(semaphore, inc=1, device_id=device, device_id_type=MESH)
+
+    for peer in beside:
+        enter((seg, peer))
+    pl.when(jnp.logical_not(late))(lambda: enter((after, me)))
+    pl.when(early)(lambda: enter((before, me)))
+    for other in row_order[:3]:
+        @pl.when(other > row)
+        def _(other=other):
+            for j in range(SIDE):
+                enter((seg, other * SIDE + lax.rem(place + j, SIDE)))
 
     loads = [
         pltpu.make_async_copy(source, target, local_sem.at[spot])
@@ -62,7 +73,13 @@
         pack_send[u] = jnp.where(keep, low, high).astype(bf16)
         edge_send[u:u + 1, :] = jnp.sum(
             jnp.where(far, low, 0.0) + jnp.where(near, high, 0.0), axis=0, keepdims=True)
-    pl.semaphore_wait(barrier, bonds + 1)
+    pl.semaphore_wait(barrier, SIDE * row + SIDE - jnp.where(early, 1, 0) + jnp.where(late, 1, 0))
+    for other in row_order[:3]:
+        @pl.when(other < row)
+        def _(other=other):
+            for j in range(SIDE):
+                enter((seg, other * SIDE + lax.rem(place + j, SIDE)), ready)
+    pl.when(late)(lambda: enter((after, me), distant))
 
     share = 8 // CHUNKS
     ring = [pltpu.make_async_remote_copy(
@@ -74,8 +91,11 @@
             src_ref=pack_send.at[part], dst_ref=pack_recv.at[part],
             send_sem=ring_send.at[c], recv_sem=ring_recv.at[c],
             device_id=(before, me), device_id_type=MESH))
-    for copy in ring:
-        copy.start()
+
+    @pl.when(jnp.logical_not(early))
+    def _():
+        for copy in ring:
+            copy.start()
 
     def unpack(u):
         half = pack_recv[u].astype(f32)
@@ -103,18 +123,22 @@
             return carry
         lax.fori_loop(0, 4, step, 0)
 
-    def scatter_copy(phase, step, source, target):
-        peer = peers[step]
-        return pltpu.make_async_remote_copy(
-            src_ref=source.at[pl.ds(pl.multiple_of(peer * rows, rows), rows), :], dst_ref=target.at[step],
-            send_sem=block_send.at[phase, step], recv_sem=block_recv.at[phase, step],
+    def remote(source, target, phase, slot, peer):
+        copy = pltpu.make_async_remote_copy(
+            src_ref=source, dst_ref=target, send_sem=block_send.at[phase, slot], recv_sem=block_recv.at[phase, slot],
             device_id=(seg, peer), device_id_type=MESH)
-
-    def image(source, vector, sent, target, phase, scale, first, more):
+        copy.start()
+        pending.append(copy)
+        return copy
+
+    def rows_of(k, column):
+        return pl.ds(pl.multiple_of((row_order[k] * SIDE + column) * rows, rows), rows)
+
+    def image(source, vector, sent, side, phase, scale, first, more):
         lanes = slice(first, 1024)
         dots = jnp.zeros((8, 128), f32)
         copies = []
-        for k in range(4):
+        for k in range(ROW):
             span = pl.ds(pl.multiple_of(row_order[k] * 256, 256), 256)
             part = jnp.dot(source[span, lanes], stacked[lanes, :], preferred_element_type=f32)
             if more:
@@ -124,10 +148,31 @@
                 part = part * scale
             partial[span, :] = part
             sent[span, :] = part.astype(bf16)
-            for step in by_row[k]:
-                copies.append(scatter_copy(phase, step, sent, target))
-                copies[-1].start()
+            for j in (2, 1, 3):
+                column = lax.rem(place + j, SIDE)
+                slot = k * 3 + j - 1
+                copies.append(remote(
+                    sent.at[rows_of(k, column), :], side.at[slot], phase, slot, row * SIDE + column))
         return total(dots), copies
+
+    def along_z(phase, copies, side, sent, target):
+        onward = []
+        for k in range(ROW):
+            value = partial[rows_of(k, place), :]
+            for copy in copies[3 * k:3 * k + 3]:
+                copy.wait_recv()
+            for slot in range(3 * k, 3 * k + 3):
+                value = value + side[slot].astype(f32)
+            if k < 3:
+                sent[k] = value.astype(bf16)
+                onward.append(remote(sent.at[k], target.at[k], phase, 12 + k, row_order[k] * SIDE + place))
+        return value, onward
+
+    def scatter_sum(value, onward, target):
+        for k in (2, 1, 0):
+            onward[k].wait_recv()
+            value = value + target[k].astype(f32)
+        return value
 
     def grow(pairs, target):
         for u in range(0, 8, 2):
@@ -140,7 +185,7 @@
             target[pl.ds(u + 1, 128, stride=8), :] = value[:, 128:]
 
     def scalar_round(phase, value):
-        scal_send[phase] = jnp.broadcast_to(value, (8, 128))
+        scal_send[phase] = jnp.broadcast_to(value, (1, 128))
         copies = []
         for step, peer in enumerate(peers):
             copies.append(pltpu.make_async_remote_copy(
@@ -154,16 +199,9 @@
     def scalar_sum(phase, copies):
         for copy in copies:
             copy.wait()
-        return jnp.sum(scal_recv[phase], axis=0)[:1, :1]
+        return jnp.sum(scal_recv[phase], axis=0)[:, :1]
 
     own = pl.ds(pl.multiple_of(me * rows, rows), rows)
-
-    def scatter_sum(copies, target):
-        value = partial[own, :]
-        for step in reversed(range(len(copies))):
-            copies[step].wait()
-            value = value + target[step].astype(f32)
-        return value
 
     loads[1].wait()
     spread[...] = start[...].astype(f32)
@@ -199,36 +237,50 @@
                 partial[span, :] = part if c == 0 else partial[span, :] + part
                 return carry
             lax.fori_loop(0, 4, add, 0)
-    ray, copies = image(coupled_1, start, send_1, recv_1, 0, None, (CHUNKS - 1) * share * 128, True)
+    ray, copies = image(coupled_1, start, send_1, side_1, 0, None, (CHUNKS - 1) * share * 128, True)
+    pl.when(row < ROW - 1)(lambda: pl.semaphore_wait(ready, SIDE * (ROW - 1 - row)))
     ray_copies = scalar_round(0, ray)
     grow([(start_t, coupled_1)], grown_11)
+    @pl.when(early)
+    def _():
+        pl.semaphore_wait(distant, 1)
+        for copy in ring:
+            copy.start()
+
+    value, onward = along_z(0, copies, side_1, sums_1, recv_1)
     rayleigh = scalar_sum(0, ray_copies) * (inverse * inverse / entries)
-    image_1 = scatter_sum(copies, recv_1)
+    image_1 = scatter_sum(value, onward, recv_1)
     block = inverse * image_1 - (rayleigh * inverse) * start[own, :].astype(f32)
     resid[own, :] = block.astype(bf16)
-    copies = []
-    for step, peer in enumerate(peers):
-        copies.append(pltpu.make_async_remote_copy(
-            src_ref=resid.at[own, :], dst_ref=resid.at[own, :],
-            send_sem=block_send.at[1, step], recv_sem=block_recv.at[1, step],
-            device_id=(seg, peer), device_id_type=MESH))
-        copies[-1].start()
+
+    def spread_out(k):
+        held = resid.at[rows_of(k, place), :]
+        return [remote(held, held, 1, k * 3 + j - 1, row * SIDE + lax.rem(place + j, SIDE)) for j in (2, 1, 3)]
+
+    mine = resid.at[own, :]
+    onward = [remote(mine, mine, 1, 12 + k, row_order[k] * SIDE + place) for k in range(3)]
+    relayed = {3: spread_out(3)}
     size_copies = scalar_round(1, total(block * block))
+    for k in (2, 1, 0):
+        onward[k].wait_recv()
+        relayed[k] = spread_out(k)
 
     for k in (3, 2, 1, 0):
-        for step in by_row[k]:
-            copies[step].wait()
+        for copy in relayed[k]:
+            copy.wait_recv()
         span = pl.ds(pl.multiple_of(row_order[k] * 256, 256), 256)
         spread[span, :] = resid[span, :].astype(f32)
         for t in range(8):
             wide[pl.ds(pl.multiple_of(row_order[k] * 32, 32), 32), t * 128:(t + 1) * 128] = (
                 spread[pl.ds(row_order[k] * 256 + t, 32, stride=8), :].astype(bf16))
+
     couple(coupled_2)
     size = jnp.sqrt(scalar_sum(1, size_copies) / entries + epsilon)
-    curve, copies = image(coupled_2, resid, send_2, recv_2, 2, 1.0 / size, 0, False)
+    curve, copies = image(coupled_2, resid, send_2, side_2, 2, 1.0 / size, 0, False)
     curve_copies = scalar_round(2, curve)
     resid_t[...] = jnp.transpose(resid[...])
     grow([(start_t, coupled_2), (resid_t, coupled_1)], grown_x)
+    value, onward = along_z(2, copies, side_2, sums_2, recv_2)
     grow([(resid_t, coupled_2)], grown_22)
     curvature = scalar_sum(2, curve_copies) / (size * size * entries)
     middle = 0.5 * (rayleigh + curvature)
@@ -242,9 +294,9 @@
     state_ref[...] = (first * start[...].astype(f32) + second * resid[...].astype(f32)).astype(bf16)
     grown_ref[...] = (first * first * grown_11[...] + first * second * grown_x[...]
                       + second * second * grown_22[...]).astype(bf16)
-    for copy in ring:
+    for copy in ring + pending:
         copy.wait_send()
-    image_ref[...] = scatter_sum(copies, recv_2)
+    image_ref[...] = scatter_sum(value, onward, recv_2)
 
 
 def write_out(state, grown, energy, image, state_out, grown_out, energy_out, image_out, sems):
@@ -291,14 +343,20 @@
                 pltpu.VMEM((128, 1024), bf16),
                 pltpu.VMEM(big, bf16),
                 pltpu.VMEM(big, bf16),
-                pltpu.VMEM((bonds - 1,) + half, bf16),
-                pltpu.VMEM((bonds - 1,) + half, bf16),
-                pltpu.VMEM(big, bf16),
-                pltpu.VMEM((3, 8, 128), f32),
-                pltpu.VMEM((3, bonds, 8, 128), f32),
+                pltpu.VMEM((12,) + half, bf16),
+                pltpu.VMEM((12,) + half, bf16),
+                pltpu.VMEM((3,) + half, bf16),
+                pltpu.VMEM((3,) + half, bf16),
+                pltpu.VMEM((3,) + half, bf16),
+                pltpu.VMEM((3,) + half, bf16),
+                pltpu.VMEM(big, bf16),
+                pltpu.VMEM((3, 1, 128), f32),
+                pltpu.VMEM((3, bonds, 1, 128), f32),
                 pltpu.VMEM(big, f32),
                 pltpu.VMEM(big, f32),
                 pltpu.VMEM(big, f32),
+                pltpu.SemaphoreType.REGULAR,
+                pltpu.SemaphoreType.REGULAR,
                 pltpu.SemaphoreType.DMA((4,)),
                 pltpu.SemaphoreType.DMA((CHUNKS + 1,)),
                 pltpu.SemaphoreType.DMA((CHUNKS + 1,)),

time: 55.9 us -> 45.1 us (0.81)
  the two profiles are of different devices: /device:TPU:1 before, /device:TPU:6 now
where the time goes in v3:
time: 45.1 us; the launch traced here: 45 us
  Pallas kernels  44.3 us (98%)
  between operations  0.64 us (1%)
    pallas_call x1, Pallas kernels, body(): pl.pallas_call(lambda *refs: kernel(segs, bonds, *refs), out_shape=(pltpu...  43 us
    pallas_call x1, Pallas kernels, body(): pl.pallas_call(write_out, out_shape=(jax.ShapeDtypeStruct(big, bf16), jax...  1.34 us

profile of v3, /device:TPU:6, one launch (start us, length us, event | category | flops | bytes accessed | tf_op | source)
XLA Modules:
  0.0 45.0 jit_solution(1718111710959386624)
XLA Ops:
  0.6 43.0 %ritz_step.1 = (bf16[1024,128]{1,0:T(8,128)(2,1)S(1)}, bf16[1024,128]{1,0:T(8,128)(2,1)S(1)}, f32[8,128]{1,0:T(8,128)S(1)}, f32[64,128]{1,0:T(8,128)S(1)}) custom-call(bf16[1024,128]{1,0:T(8,128)(2,1)} %bitcast.7, bf16[1024,128]{1,0:T(8,128)(2,1)} %bitcast.8, bf16[8,8,8,8]{3,2,1,0:T(8,128)(2,1)} %bitcast.10, bf16[1024,128]{1,0:T(8,128)(2,1)} %bitcast.9), custom_call_target="tpu_custom_call" | custom-call | tf_op jit(solution)/shard_map/ritz_step/pallas_call | solution.py:321
  43.6 1.3 %write_out.1 = (bf16[1024,128]{1,0:T(8,128)(2,1)}, bf16[1024,128]{1,0:T(8,128)(2,1)}, f32[1]{0:T(128)}, f32[64,128]{1,0:T(8,128)}) custom-call(bf16[1024,128]{1,0:T(8,128)(2,1)S(1)} %get-tuple-element.12.state, bf16[1024,128]{1,0:T(8,128)(2,1)S(1)} %get-tuple-element.13.grown, f32[8,128]{1,0:T(8,128)S(1)} %get-tuple-element.14.energy, ...), custom_call_target="tpu_custom_call" | custom-call | tf_op jit(solution)/shard_map/write_out/pallas_call | solution.py:373

commit v4 on v3

--- a/solution.py
+++ b/solution.py
@@ -9,7 +9,7 @@
 MESH = pl.DeviceIdType.MESH
 f32, bf16 = jnp.float32, jnp.bfloat16
 ROW, SIDE = 4, 4
-CHUNKS = 4
+CHUNKS = 2
 
 
 def total(value):
@@ -36,23 +36,6 @@
                 peers.append(other * SIDE + lax.rem(place + j, SIDE))
     pending = []
 
-    early, late = lax.rem(seg, 8) == 0, lax.rem(seg, 8) == 7
-    beside = [row * SIDE + lax.rem(place + j, SIDE) for j in range(1, SIDE)]
-    barrier = pltpu.get_barrier_semaphore()
-
-    def enter(device, semaphore=barrier):
-        pl.semaphore_signal(semaphore, inc=1, device_id=device, device_id_type=MESH)
-
-    for peer in beside:
-        enter((seg, peer))
-    pl.when(jnp.logical_not(late))(lambda: enter((after, me)))
-    pl.when(early)(lambda: enter((before, me)))
-    for other in row_order[:3]:
-        @pl.when(other > row)
-        def _(other=other):
-            for j in range(SIDE):
-                enter((seg, other * SIDE + lax.rem(place + j, SIDE)))
-
     loads = [
         pltpu.make_async_copy(source, target, local_sem.at[spot])
         for spot, (source, target) in enumerate(
@@ -60,6 +43,17 @@
     ]
     for load in loads:
         load.start()
+
+    early, late = lax.rem(seg, 8) == 0, lax.rem(seg, 8) == 7
+    barrier = pltpu.get_barrier_semaphore()
+
+    def enter(device, semaphore=barrier):
+        pl.semaphore_signal(semaphore, inc=1, device_id=device, device_id_type=MESH)
+
+    pl.when(jnp.logical_not(late))(lambda: enter((after, me)))
+    pl.when(early)(lambda: enter((before, me)))
+    for peer in peers:
+        pl.when(peer > me)(lambda peer=peer: enter((seg, peer)))
 
     up = lax.broadcasted_iota(jnp.int32, (64, 128), 0)
     lane = lax.broadcasted_iota(jnp.int32, (64, 128), 1)
@@ -73,12 +67,8 @@
         pack_send[u] = jnp.where(keep, low, high).astype(bf16)
         edge_send[u:u + 1, :] = jnp.sum(
             jnp.where(far, low, 0.0) + jnp.where(near, high, 0.0), axis=0, keepdims=True)
-    pl.semaphore_wait(barrier, SIDE * row + SIDE - jnp.where(early, 1, 0) + jnp.where(late, 1, 0))
-    for other in row_order[:3]:
-        @pl.when(other < row)
-        def _(other=other):
-            for j in range(SIDE):
-                enter((seg, other * SIDE + lax.rem(place + j, SIDE)), ready)
+    ahead = me + 1 - jnp.where(early, 1, 0) + jnp.where(late, 1, 0)
+    pl.when(ahead > 0)(lambda: pl.semaphore_wait(barrier, ahead))
     pl.when(late)(lambda: enter((after, me), distant))
 
     share = 8 // CHUNKS
@@ -97,6 +87,9 @@
         for copy in ring:
             copy.start()
 
+    for peer in peers:
+        pl.when(peer < me)(lambda peer=peer: enter((seg, peer), ready))
+
     def unpack(u):
         half = pack_recv[u].astype(f32)
         turned = jnp.transpose(jnp.concatenate([half, half], axis=0))
@@ -107,7 +100,7 @@
         stacked[u * 128 + 64:u * 128 + 128, :] = low.astype(bf16)
 
     def couple(target):
-        def step(i, carry):
+        def step(i):
             mixed = jnp.dot(left[pl.ds(i * 256, 256), :], wide[...], preferred_element_type=f32)
             shaped = jnp.stack([mixed[:, t * 128:(t + 1) * 128].reshape(32, 8, 128) for t in range(8)], axis=1)
             shaped = shaped.reshape(2048, 128).astype(bf16)
@@ -120,8 +113,8 @@
                     for u in range(8):
                         target[pl.ds(i * 256 + g * 64 + h * 32, 32), u * 128:(u + 1) * 128] = (
                             half[:, u].reshape(32, 128).astype(bf16))
-            return carry
-        lax.fori_loop(0, 4, step, 0)
+        for i in range(4):
+            step(i)
 
     def remote(source, target, phase, slot, peer):
         copy = pltpu.make_async_remote_copy(
@@ -237,8 +230,8 @@
                 partial[span, :] = part if c == 0 else partial[span, :] + part
                 return carry
             lax.fori_loop(0, 4, add, 0)
+    pl.when(me < bonds - 1)(lambda: pl.semaphore_wait(ready, bonds - 1 - me))
     ray, copies = image(coupled_1, start, send_1, side_1, 0, None, (CHUNKS - 1) * share * 128, True)
-    pl.when(row < ROW - 1)(lambda: pl.semaphore_wait(ready, SIDE * (ROW - 1 - row)))
     ray_copies = scalar_round(0, ray)
     grow([(start_t, coupled_1)], grown_11)
     @pl.when(early)
@@ -299,14 +292,16 @@
     image_ref[...] = scatter_sum(value, onward, recv_2)
 
 
-def write_out(state, grown, energy, image, state_out, grown_out, energy_out, image_out, sems):
+def write_out(state, grown, energy, image, state_out, grown_out, energy_out, image_out, lowest, sems):
     copies = [
         pltpu.make_async_copy(source, target, sems.at[spot])
         for spot, (source, target) in enumerate(((state, state_out), (grown, grown_out), (image, image_out)))
     ]
     for copy in copies:
         copy.start()
-    energy_out[0] = energy[0, 0]
+    lowest[0] = energy[0, 0]
+    copies.append(pltpu.make_async_copy(lowest, energy_out, sems.at[3]))
+    copies[3].start()
     for copy in copies:
         copy.wait()
 
@@ -379,8 +374,8 @@
                 jax.ShapeDtypeStruct(half, f32),
             ),
             in_specs=[vmem] * 4,
-            out_specs=(anywhere, anywhere, pl.BlockSpec(memory_space=pltpu.SMEM), anywhere),
-            scratch_shapes=[pltpu.SemaphoreType.DMA((3,))],
+            out_specs=(anywhere,) * 4,
+            scratch_shapes=[pltpu.SMEM((1,), f32), pltpu.SemaphoreType.DMA((4,))],
             compiler_params=pltpu.CompilerParams(vmem_limit_bytes=8 * 1024 * 1024),
             name="write_out",
         )(*results)

time: 45.1 us -> 44 us (0.976)
  Pallas kernels: 44.3 us -> 43 us
    pallas_call x1, Pallas kernels: 43 us -> 42.2 us  [body(): pl.pallas_call(lambda *refs: kernel(segs, bonds, *refs), out_shape=(pltpu...]
    pallas_call x1, Pallas kernels: 1.34 us -> 0.84 us  [body(): pl.pallas_call(write_out, out_shape=(jax.ShapeDtypeStruct(big, bf16), jax...]
where the time goes in v4:
time: 44 us; the launch traced here: 43.7 us
  Pallas kernels  43 us (98%)
  between operations  0.64 us (1%)
    pallas_call x1, Pallas kernels, body(): pl.pallas_call(lambda *refs: kernel(segs, bonds, *refs), out_shape=(pltpu...  42.2 us

profile of v4, /device:TPU:6, one launch (start us, length us, event | category | flops | bytes accessed | tf_op | source)
XLA Modules:
  0.0 43.7 jit_solution(11304921405204725693)
XLA Ops:
  0.6 42.2 %ritz_step.1 = (bf16[1024,128]{1,0:T(8,128)(2,1)S(1)}, bf16[1024,128]{1,0:T(8,128)(2,1)S(1)}, f32[8,128]{1,0:T(8,128)S(1)}, f32[64,128]{1,0:T(8,128)S(1)}) custom-call(bf16[1024,128]{1,0:T(8,128)(2,1)} %bitcast.7, bf16[1024,128]{1,0:T(8,128)(2,1)} %bitcast.8, bf16[8,8,8,8]{3,2,1,0:T(8,128)(2,1)} %bitcast.10, bf16[1024,128]{1,0:T(8,128)(2,1)} %bitcast.9), custom_call_target="tpu_custom_call" | custom-call | tf_op jit(solution)/shard_map/ritz_step/pallas_call | solution.py:316
  42.8 0.8 %write_out.1 = (bf16[1024,128]{1,0:T(8,128)(2,1)}, bf16[1024,128]{1,0:T(8,128)(2,1)}, f32[1]{0:T(128)}, f32[64,128]{1,0:T(8,128)}) custom-call(bf16[1024,128]{1,0:T(8,128)(2,1)S(1)} %get-tuple-element.12.state, bf16[1024,128]{1,0:T(8,128)(2,1)S(1)} %get-tuple-element.13.grown, f32[8,128]{1,0:T(8,128)S(1)} %get-tuple-element.14.energy, ...), custom_call_target="tpu_custom_call" | custom-call | tf_op jit(solution)/shard_map/write_out/pallas_call | solution.py:368

commit v5 on v4

--- a/solution.py
+++ b/solution.py
@@ -99,22 +99,19 @@
         stacked[u * 128:u * 128 + 64, :] = top.astype(bf16)
         stacked[u * 128 + 64:u * 128 + 128, :] = low.astype(bf16)
 
-    def couple(target):
-        def step(i):
-            mixed = jnp.dot(left[pl.ds(i * 256, 256), :], wide[...], preferred_element_type=f32)
-            shaped = jnp.stack([mixed[:, t * 128:(t + 1) * 128].reshape(32, 8, 128) for t in range(8)], axis=1)
-            shaped = shaped.reshape(2048, 128).astype(bf16)
-            for g in range(4):
-                pair = jnp.concatenate(
-                    [shaped[g * 512:g * 512 + 256], shaped[g * 512 + 256:g * 512 + 512]], axis=1)
-                out = jnp.dot(coupler[...], pair, preferred_element_type=f32)
-                for h in range(2):
-                    half = out[:, h * 128:(h + 1) * 128].reshape(4, 8, 8, 128)
-                    for u in range(8):
-                        target[pl.ds(i * 256 + g * 64 + h * 32, 32), u * 128:(u + 1) * 128] = (
-                            half[:, u].reshape(32, 128).astype(bf16))
-        for i in range(4):
-            step(i)
+    def couple(i, target):
+        mixed = jnp.dot(left[pl.ds(i * 256, 256), :], wide[...], preferred_element_type=f32)
+        shaped = jnp.stack([mixed[:, t * 128:(t + 1) * 128].reshape(32, 8, 128) for t in range(8)], axis=1)
+        shaped = shaped.reshape(2048, 128).astype(bf16)
+        for g in range(4):
+            pair = jnp.concatenate(
+                [shaped[g * 512:g * 512 + 256], shaped[g * 512 + 256:g * 512 + 512]], axis=1)
+            out = jnp.dot(coupler[...], pair, preferred_element_type=f32)
+            for h in range(2):
+                half = out[:, h * 128:(h + 1) * 128].reshape(4, 8, 8, 128)
+                for u in range(8):
+                    target[pl.ds(i * 256 + g * 64 + h * 32, 32), u * 128:(u + 1) * 128] = (
+                        half[:, u].reshape(32, 128).astype(bf16))
 
     def remote(source, target, phase, slot, peer):
         copy = pltpu.make_async_remote_copy(
@@ -133,6 +130,8 @@
         copies = []
         for k in range(ROW):
             span = pl.ds(pl.multiple_of(row_order[k] * 256, 256), 256)
+            if not more:
+                couple(row_order[k], source)
             part = jnp.dot(source[span, lanes], stacked[lanes, :], preferred_element_type=f32)
             if more:
                 part = part + partial[span, :]
@@ -215,7 +214,8 @@
     lane_group = lax.broadcasted_iota(jnp.int32, (256, 256), 1) // 64
     coupler[...] = jnp.where(row_group == lane_group, tall, 0.0).astype(bf16)
     loads[2].wait()
-    couple(coupled_1)
+    for i in range(ROW):
+        couple(i, coupled_1)
     start_t[...] = jnp.transpose(start[...])
 
     ring[0].wait_recv()
@@ -267,7 +267,6 @@
             wide[pl.ds(pl.multiple_of(row_order[k] * 32, 32), 32), t * 128:(t + 1) * 128] = (
                 spread[pl.ds(row_order[k] * 256 + t, 32, stride=8), :].astype(bf16))
 
-    couple(coupled_2)
     size = jnp.sqrt(scalar_sum(1, size_copies) / entries + epsilon)
     curve, copies = image(coupled_2, resid, send_2, side_2, 2, 1.0 / size, 0, False)
     curve_copies = scalar_round(2, curve)

time: 44 us -> 43.4 us (0.986)
  Pallas kernels: 43 us -> 42.1 us
    pallas_call x1, Pallas kernels: 42.2 us -> 41.3 us  [body(): pl.pallas_call(lambda *refs: kernel(segs, bonds, *refs), out_shape=(pltpu...]
where the time goes in v5:
time: 43.4 us; the launch traced here: 42.8 us
  Pallas kernels  42.1 us (97%)
  between operations  0.64 us (1%)
    pallas_call x1, Pallas kernels, body(): pl.pallas_call(lambda *refs: kernel(segs, bonds, *refs), out_shape=(pltpu...  41.3 us

profile of v5, /device:TPU:6, one launch (start us, length us, event | category | flops | bytes accessed | tf_op | source)
XLA Modules:
  0.0 42.8 jit_solution(9122600363901949147)
XLA Ops:
  0.6 41.3 %ritz_step.1 = (bf16[1024,128]{1,0:T(8,128)(2,1)S(1)}, bf16[1024,128]{1,0:T(8,128)(2,1)S(1)}, f32[8,128]{1,0:T(8,128)S(1)}, f32[64,128]{1,0:T(8,128)S(1)}) custom-call(bf16[1024,128]{1,0:T(8,128)(2,1)} %bitcast.7, bf16[1024,128]{1,0:T(8,128)(2,1)} %bitcast.8, bf16[8,8,8,8]{3,2,1,0:T(8,128)(2,1)} %bitcast.10, bf16[1024,128]{1,0:T(8,128)(2,1)} %bitcast.9), custom_call_target="tpu_custom_call" | custom-call | tf_op jit(solution)/shard_map/ritz_step/pallas_call | solution.py:315
  42.0 0.8 %write_out.1 = (bf16[1024,128]{1,0:T(8,128)(2,1)}, bf16[1024,128]{1,0:T(8,128)(2,1)}, f32[1]{0:T(128)}, f32[64,128]{1,0:T(8,128)}) custom-call(bf16[1024,128]{1,0:T(8,128)(2,1)S(1)} %get-tuple-element.12.state, bf16[1024,128]{1,0:T(8,128)(2,1)S(1)} %get-tuple-element.13.grown, f32[8,128]{1,0:T(8,128)S(1)} %get-tuple-element.14.energy, ...), custom_call_target="tpu_custom_call" | custom-call | tf_op jit(solution)/shard_map/write_out/pallas_call | solution.py:367
